TPU v7x, 32 devices: a whole 2x2x4 slice. The times are simulated.
32 devices in a mesh: dp: 4 (over z), seq: 8 (over y, x, core).
Axes of the slice: x: 2, y: 2, z: 4, core: 2. Of those that a mesh axis runs over, the one named last changes fastest.
Arguments:
- tokens: bfloat16 [16, 2048, 768], P('dp', 'seq'), may hold values from -6 to 6
- token_types: int32 [16, 2048], P('dp'), may hold values 0 or 1
- segment_ids: int32 [16, 2048], P('dp'), may hold values from 0 to 7, never falling along the last dimension, each value on 1 to 1024 neighbouring positions
- query_weight: bfloat16 [1536, 1536], P(('dp', 'seq')), may hold values from -0.21875 to 0.21875
- query_bias: bfloat16 [3072], P(('dp', 'seq')), may hold values from -3 to 3
- key_weight: bfloat16 [768, 768], P(('dp', 'seq')), may hold values from -0.21875 to 0.21875
- value_weight: bfloat16 [768, 768], P(('dp', 'seq')), may hold values from -0.21875 to 0.21875
- value_bias: bfloat16 [768], P(('dp', 'seq')), may hold values from -0.29882812 to 0.29882812
- out_weight: bfloat16 [768, 768], P(('dp', 'seq')), may hold values from -1.75 to 1.75
- out_bias: bfloat16 [768], P(('dp', 'seq')), may hold values from -1.1953125 to 1.1953125
- norm1_gain: bfloat16 [768], P(('dp', 'seq')), may hold values from 0.5 to 1.5
- norm1_bias: bfloat16 [768], P(('dp', 'seq')), may hold values from -1.1953125 to 1.1953125
- up_weight: bfloat16 [768, 3072], P(('dp', 'seq')), may hold values from -0.21875 to 0.21875
- up_bias: bfloat16 [3072], P(('dp', 'seq')), may hold values from -1.796875 to 1.796875
- down_weight: bfloat16 [3072, 768], P(('dp', 'seq')), may hold values from -0.109375 to 0.109375
- down_bias: bfloat16 [768], P(('dp', 'seq')), may hold values from -1.1953125 to 1.1953125
- norm2_gain: bfloat16 [768], P(('dp', 'seq')), may hold values from 0.5 to 1.5
- norm2_bias: bfloat16 [768], P(('dp', 'seq')), may hold values from -1.1953125 to 1.1953125
- cotangent: bfloat16 [16, 2048, 768], P('dp', 'seq'), may hold values from -6 to 6
Outputs:
- layer_output: bfloat16 [16, 2048, 768], P('dp', 'seq')
- input_grad: float32 [16, 2048, 768], P('dp', 'seq')
- grad_query_weight: float32 [1536, 1536], P(('dp', 'seq'))
- grad_query_bias: float32 [3072], P(('dp', 'seq'))
- grad_key_weight: float32 [768, 768], P(('dp', 'seq'))
- grad_value_weight: float32 [768, 768], P(('dp', 'seq'))
- grad_value_bias: float32 [768], P(('dp', 'seq'))
- grad_out_weight: float32 [768, 768], P(('dp', 'seq'))
- grad_out_bias: float32 [768], P(('dp', 'seq'))
- grad_norm1_gain: float32 [768], P(('dp', 'seq'))
- grad_norm1_bias: float32 [768], P(('dp', 'seq'))
- grad_up_weight: float32 [768, 3072], P(('dp', 'seq'))
- grad_up_bias: float32 [3072], P(('dp', 'seq'))
- grad_down_weight: float32 [3072, 768], P(('dp', 'seq'))
- grad_down_bias: float32 [768], P(('dp', 'seq'))
- grad_norm2_gain: float32 [768], P(('dp', 'seq'))
- grad_norm2_bias: float32 [768], P(('dp', 'seq'))
All inputs are finite; a program needn't handle non-finite values. No bound on the sum of `token_types` on one device may be relied on, other than what follows from the above.
Results may differ from a plain program's by a relative error of at most 0.02.
Values may be sent and summed in bfloat16 or wider, within the bound.
No kernel may reach another device: no remote copies, remote signals or barrier semaphores. Data moves between devices by JAX's collectives and lax.ppermute only.
A program may use at most 256 MiB of HBM per device.

v0:
```python
import math

import jax
import jax.numpy as jnp
from jax import lax
from jax.sharding import PartitionSpec as P

HEAD_DIM = 64


NORM_EPS = 1e-12
MASKED = -1e30


def layer_norm(hidden, gain_vec, shift_vec):
    center = hidden - jnp.mean(hidden, axis=-1, keepdims=True)
    spread = jnp.mean(center * center, axis=-1, keepdims=True)
    return center * lax.rsqrt(spread + NORM_EPS) * gain_vec + shift_vec


def gelu_exact(pre_act):
    return jax.nn.gelu(pre_act, approximate=False)


def dot_plain(left_op, right_op):
    return jnp.dot(left_op, right_op, preferred_element_type=jnp.float32)


def dot_rows(left_op, right_op):
    return lax.dot_general(
        left_op, right_op, (((0,), (0,)), ((), ())), preferred_element_type=jnp.float32
    )


def dot_cols(left_op, right_op):
    return lax.dot_general(
        left_op, right_op, (((1,), (1,)), ((), ())), preferred_element_type=jnp.float32
    )


def key_side(kv_part, kind_part, model_width, head_count):
    seq_count, key_count = (kv_part.shape[0], kv_part.shape[1])
    key_rows = kv_part[..., :model_width].reshape(
        seq_count, key_count, head_count, model_width // head_count
    )
    value_rows = kv_part[..., model_width:].reshape(
        seq_count, key_count, head_count, model_width // head_count
    )
    entity = kind_part[:, :, None, None].astype(jnp.bfloat16)
    joined = jnp.concatenate([key_rows * (1 - entity), key_rows * entity], axis=-1)
    return (joined, value_rows)


def block_scores(queries, joined, query_seg, key_seg, score_scale):
    raw_scores = jnp.einsum("sqhc,skhc->sqhk", queries, joined, preferred_element_type=jnp.float32)
    same_doc = (query_seg[:, :, None] == key_seg[:, None, :])[:, :, None, :]
    return (jnp.where(same_doc, score_scale * raw_scores, MASKED), same_doc)


def fold_keys(
    state_in,
    kv_piece,
    queries,
    query_seg,
    segment_ids,
    token_types,
    model_width,
    head_count,
    score_scale,
):
    key_count = kv_piece.shape[1]
    block_size = math.gcd(key_count, 256)

    def one_block(block_index, running):
        run_acc, run_max, run_sum = running
        block_start = block_index * block_size
        kv_part = lax.dynamic_slice_in_dim(kv_piece, block_start, block_size, 1)
        key_seg = lax.dynamic_slice_in_dim(segment_ids, block_start, block_size, 1)
        kind_part = lax.dynamic_slice_in_dim(token_types, block_start, block_size, 1)
        joined, value_rows = key_side(kv_part, kind_part, model_width, head_count)
        scores, same_doc = block_scores(queries, joined, query_seg, key_seg, score_scale)
        new_max = jnp.maximum(run_max, jnp.max(scores, axis=-1))
        factor = jnp.exp(run_max - new_max)
        exp_terms = jnp.where(same_doc, jnp.exp(scores - new_max[..., None]), 0.0)
        run_sum = run_sum * factor + jnp.sum(exp_terms, axis=-1)
        run_acc = run_acc * factor[..., None] + jnp.einsum(
            "sqhk,skhd->sqhd",
            exp_terms.astype(jnp.bfloat16),
            value_rows,
            preferred_element_type=jnp.float32,
        )
        return (run_acc, new_max, run_sum)

    return lax.fori_loop(0, key_count // block_size, one_block, state_in)


def grad_scores(
    queries,
    grad_attn,
    log_total,
    row_delta,
    query_seg,
    kv_part,
    key_seg,
    kind_part,
    model_width,
    head_count,
    score_scale,
):
    joined, value_rows = key_side(kv_part, kind_part, model_width, head_count)
    scores, same_doc = block_scores(queries, joined, query_seg, key_seg, score_scale)
    probs = jnp.where(same_doc, jnp.exp(scores - log_total[..., None]), 0.0)
    grad_probs = jnp.einsum(
        "sqhd,skhd->sqhk", grad_attn, value_rows, preferred_element_type=jnp.float32
    )
    grad_raw = (score_scale * probs * (grad_probs - row_delta[..., None])).astype(jnp.bfloat16)
    return (grad_raw, probs.astype(jnp.bfloat16), joined)


def key_grads_block(grad_raw, probs_low, queries, grad_attn, kind_part, model_width):
    grad_joined = jnp.einsum(
        "sqhk,sqhc->skhc", grad_raw, queries, preferred_element_type=jnp.float32
    )
    entity = kind_part[:, :, None, None].astype(jnp.float32)
    half_width = grad_joined.shape[-1] // 2
    grad_key = (
        grad_joined[..., :half_width] * (1.0 - entity) + grad_joined[..., half_width:] * entity
    )
    grad_value = jnp.einsum(
        "sqhk,sqhd->skhd", probs_low, grad_attn, preferred_element_type=jnp.float32
    )
    seq_count, key_count = (grad_key.shape[0], grad_key.shape[1])
    return jnp.concatenate(
        [
            grad_key.reshape(seq_count, key_count, model_width),
            grad_value.reshape(seq_count, key_count, model_width),
        ],
        axis=-1,
    )


def per_device(
    tokens,
    token_types,
    segment_ids,
    query_weight,
    query_bias,
    key_weight,
    value_weight,
    value_bias,
    out_weight,
    out_bias,
    norm1_gain,
    norm1_bias,
    up_weight,
    up_bias,
    down_weight,
    down_bias,
    norm2_gain,
    norm2_bias,
    cotangent,
):
    seq_count, own_rows, model_width = tokens.shape
    length = segment_ids.shape[1]
    head_count = model_width // HEAD_DIM
    score_scale = 1.0 / math.sqrt(HEAD_DIM)
    token_count = seq_count * own_rows
    offset = lax.axis_index("seq") * own_rows
    own_seg = lax.dynamic_slice_in_dim(segment_ids, offset, own_rows, 1)
    own_kinds = lax.dynamic_slice_in_dim(token_types, offset, own_rows, 1)
    entity_col = own_kinds.reshape(token_count, 1).astype(jnp.float32)
    word_col = 1.0 - entity_col
    gathered = (
        lax.all_gather(query_weight, ("dp", "seq"), axis=0, tiled=True),
        lax.all_gather(query_bias, ("dp", "seq"), axis=0, tiled=True),
        lax.all_gather(key_weight, ("dp", "seq"), axis=0, tiled=True),
        lax.all_gather(value_weight, ("dp", "seq"), axis=0, tiled=True),
        lax.all_gather(value_bias, ("dp", "seq"), axis=0, tiled=True),
        lax.all_gather(out_weight, ("dp", "seq"), axis=0, tiled=True),
        lax.all_gather(out_bias, ("dp", "seq"), axis=0, tiled=True),
        lax.all_gather(norm1_gain, ("dp", "seq"), axis=0, tiled=True),
        lax.all_gather(norm1_bias, ("dp", "seq"), axis=0, tiled=True),
        lax.all_gather(up_weight, ("dp", "seq"), axis=0, tiled=True),
        lax.all_gather(up_bias, ("dp", "seq"), axis=0, tiled=True),
        lax.all_gather(down_weight, ("dp", "seq"), axis=0, tiled=True),
        lax.all_gather(down_bias, ("dp", "seq"), axis=0, tiled=True),
        lax.all_gather(norm2_gain, ("dp", "seq"), axis=0, tiled=True),
        lax.all_gather(norm2_bias, ("dp", "seq"), axis=0, tiled=True),
    )
    (
        m_query,
        v_query,
        m_key,
        m_value,
        v_value,
        m_out,
        v_out,
        v_gain_one,
        v_shift_one,
        m_up,
        v_up,
        m_down,
        v_down,
        v_gain_two,
        v_shift_two,
    ) = gathered
    bias_query = v_query.astype(jnp.float32)
    bias_value = v_value.astype(jnp.float32)
    bias_out = v_out.astype(jnp.float32)
    gain_one = v_gain_one.astype(jnp.float32)
    shift_one = v_shift_one.astype(jnp.float32)
    bias_up = v_up.astype(jnp.float32)
    bias_down = v_down.astype(jnp.float32)
    gain_two = v_gain_two.astype(jnp.float32)
    shift_two = v_shift_two.astype(jnp.float32)
    flat_tokens = tokens.reshape(token_count, model_width)
    stacked = jnp.concatenate(
        [
            flat_tokens * word_col.astype(jnp.bfloat16),
            flat_tokens * entity_col.astype(jnp.bfloat16),
        ],
        axis=1,
    )
    query_full = (
        dot_plain(stacked, m_query)
        + word_col * bias_query[: 2 * model_width]
        + entity_col * bias_query[2 * model_width :]
    )
    queries = query_full.astype(jnp.bfloat16).reshape(seq_count, own_rows, head_count, 2 * HEAD_DIM)
    start_state = (
        jnp.zeros((seq_count, own_rows, head_count, HEAD_DIM), jnp.float32),
        jnp.full((seq_count, own_rows, head_count), MASKED, jnp.float32),
        jnp.zeros((seq_count, own_rows, head_count), jnp.float32),
    )
    key_low = dot_plain(flat_tokens, m_key).astype(jnp.bfloat16)
    value_low = (dot_plain(flat_tokens, m_value) + bias_value).astype(jnp.bfloat16)
    local_kv = jnp.concatenate([key_low, value_low], axis=1).reshape(
        seq_count, own_rows, 2 * model_width
    )
    run_acc, run_max, run_sum = fold_keys(
        start_state,
        lax.all_gather(local_kv, "seq", axis=1, tiled=True),
        queries,
        own_seg,
        segment_ids,
        token_types,
        model_width,
        head_count,
        score_scale,
    )
    attention = run_acc / run_sum[..., None]
    log_total = run_max + jnp.log(run_sum)
    attn_low = attention.reshape(token_count, model_width).astype(jnp.bfloat16)
    first_sum = flat_tokens.astype(jnp.float32) + dot_plain(attn_low, m_out) + bias_out
    normed, back_one = jax.vjp(layer_norm, first_sum, gain_one, shift_one)
    normed_low = normed.astype(jnp.bfloat16)
    up_value = dot_plain(normed_low, m_up) + bias_up
    activated, back_act = jax.vjp(gelu_exact, up_value)
    act_low = activated.astype(jnp.bfloat16)
    second_sum = normed + dot_plain(act_low, m_down) + bias_down
    output, back_two = jax.vjp(layer_norm, second_sum, gain_two, shift_two)
    back_query, back_key, back_value, back_out, back_up, back_down = (
        lax.all_gather(query_weight, ("dp", "seq"), axis=0, tiled=True),
        lax.all_gather(key_weight, ("dp", "seq"), axis=0, tiled=True),
        lax.all_gather(value_weight, ("dp", "seq"), axis=0, tiled=True),
        lax.all_gather(out_weight, ("dp", "seq"), axis=0, tiled=True),
        lax.all_gather(up_weight, ("dp", "seq"), axis=0, tiled=True),
        lax.all_gather(down_weight, ("dp", "seq"), axis=0, tiled=True),
    )
    grad_output = cotangent.reshape(token_count, model_width).astype(jnp.float32)
    grad_second, grad_gain_two, grad_shift_two = back_two(grad_output)
    grad_branch_two = grad_second.astype(jnp.bfloat16)
    grad_down_bias = jnp.sum(grad_branch_two.astype(jnp.float32), axis=0)
    grad_down = dot_rows(act_low, grad_branch_two)
    (grad_pre,) = back_act(dot_cols(grad_branch_two, back_down))
    grad_up_low = grad_pre.astype(jnp.bfloat16)
    grad_up_bias = jnp.sum(grad_up_low.astype(jnp.float32), axis=0)
    grad_up = dot_rows(normed_low, grad_up_low)
    grad_normed = grad_second + dot_cols(grad_up_low, back_up)
    grad_first, grad_gain_one, grad_shift_one = back_one(grad_normed)
    grad_branch_one = grad_first.astype(jnp.bfloat16)
    grad_out_bias = jnp.sum(grad_branch_one.astype(jnp.float32), axis=0)
    grad_out = dot_rows(attn_low, grad_branch_one)
    grad_attn = (
        dot_cols(grad_branch_one, back_out)
        .astype(jnp.bfloat16)
        .reshape(seq_count, own_rows, head_count, HEAD_DIM)
    )
    row_delta = jnp.sum(grad_attn.astype(jnp.float32) * attention, axis=-1)
    whole_kv = lax.all_gather(local_kv, "seq", axis=1, tiled=True)
    block_size = math.gcd(length, 256)
    query_zero = jnp.zeros((seq_count, own_rows, head_count, 2 * HEAD_DIM), jnp.float32)

    def back_block(block_index, running):
        grad_query_acc, grad_kv_all = running
        block_start = block_index * block_size
        kv_part = lax.dynamic_slice_in_dim(whole_kv, block_start, block_size, 1)
        key_seg = lax.dynamic_slice_in_dim(segment_ids, block_start, block_size, 1)
        kind_part = lax.dynamic_slice_in_dim(token_types, block_start, block_size, 1)
        grad_raw, probs_low, joined = grad_scores(
            queries,
            grad_attn,
            log_total,
            row_delta,
            own_seg,
            kv_part,
            key_seg,
            kind_part,
            model_width,
            head_count,
            score_scale,
        )
        grad_query_acc = grad_query_acc + jnp.einsum(
            "sqhk,skhc->sqhc", grad_raw, joined, preferred_element_type=jnp.float32
        )
        kv_block = key_grads_block(grad_raw, probs_low, queries, grad_attn, kind_part, model_width)
        grad_kv_all = lax.dynamic_update_slice_in_dim(grad_kv_all, kv_block, block_start, 1)
        return (grad_query_acc, grad_kv_all)

    grad_query_acc, grad_kv_all = lax.fori_loop(
        0,
        length // block_size,
        back_block,
        (query_zero, jnp.zeros((seq_count, length, 2 * model_width), jnp.float32)),
    )
    grad_kv_own = lax.psum_scatter(
        grad_kv_all.astype(jnp.bfloat16), "seq", scatter_dimension=1, tiled=True
    ).astype(jnp.float32)
    grad_key_low = (
        grad_kv_own[..., :model_width].reshape(token_count, model_width).astype(jnp.bfloat16)
    )
    grad_value_low = (
        grad_kv_own[..., model_width:].reshape(token_count, model_width).astype(jnp.bfloat16)
    )
    grad_query_low = grad_query_acc.reshape(token_count, 2 * model_width).astype(jnp.bfloat16)
    query_grad32 = grad_query_low.astype(jnp.float32)
    grad_query = dot_rows(stacked, grad_query_low)
    grad_query_bias = jnp.concatenate(
        [jnp.sum(word_col * query_grad32, axis=0), jnp.sum(entity_col * query_grad32, axis=0)]
    )
    grad_key = dot_rows(flat_tokens, grad_key_low)
    grad_value = dot_rows(flat_tokens, grad_value_low)
    grad_value_bias = jnp.sum(grad_value_low.astype(jnp.float32), axis=0)
    grad_stacked = dot_cols(grad_query_low, back_query)
    input_grad = (
        grad_first
        + grad_stacked[:, :model_width] * word_col
        + grad_stacked[:, model_width:] * entity_col
        + dot_cols(grad_key_low, back_key)
        + dot_cols(grad_value_low, back_value)
    )
    weight_grads = (
        lax.psum_scatter(grad_query, ("dp", "seq"), scatter_dimension=0, tiled=True),
        lax.psum_scatter(grad_query_bias, ("dp", "seq"), scatter_dimension=0, tiled=True),
        lax.psum_scatter(grad_key, ("dp", "seq"), scatter_dimension=0, tiled=True),
        lax.psum_scatter(grad_value, ("dp", "seq"), scatter_dimension=0, tiled=True),
        lax.psum_scatter(grad_value_bias, ("dp", "seq"), scatter_dimension=0, tiled=True),
        lax.psum_scatter(grad_out, ("dp", "seq"), scatter_dimension=0, tiled=True),
        lax.psum_scatter(grad_out_bias, ("dp", "seq"), scatter_dimension=0, tiled=True),
        lax.psum_scatter(grad_gain_one, ("dp", "seq"), scatter_dimension=0, tiled=True),
        lax.psum_scatter(grad_shift_one, ("dp", "seq"), scatter_dimension=0, tiled=True),
        lax.psum_scatter(grad_up, ("dp", "seq"), scatter_dimension=0, tiled=True),
        lax.psum_scatter(grad_up_bias, ("dp", "seq"), scatter_dimension=0, tiled=True),
        lax.psum_scatter(grad_down, ("dp", "seq"), scatter_dimension=0, tiled=True),
        lax.psum_scatter(grad_down_bias, ("dp", "seq"), scatter_dimension=0, tiled=True),
        lax.psum_scatter(grad_gain_two, ("dp", "seq"), scatter_dimension=0, tiled=True),
        lax.psum_scatter(grad_shift_two, ("dp", "seq"), scatter_dimension=0, tiled=True),
    )
    return (
        output.astype(jnp.bfloat16).reshape(seq_count, own_rows, model_width),
        input_grad.reshape(seq_count, own_rows, model_width),
    ) + tuple(weight_grads)


def solution(mesh):
    in_specs = (
        P("dp", "seq", None),
        P("dp", None),
        P("dp", None),
        P(("dp", "seq"), None),
        P(("dp", "seq")),
        P(("dp", "seq"), None),
        P(("dp", "seq"), None),
        P(("dp", "seq")),
        P(("dp", "seq"), None),
        P(("dp", "seq")),
        P(("dp", "seq")),
        P(("dp", "seq")),
        P(("dp", "seq"), None),
        P(("dp", "seq")),
        P(("dp", "seq"), None),
        P(("dp", "seq")),
        P(("dp", "seq")),
        P(("dp", "seq")),
        P("dp", "seq", None),
    )
    out_specs = (
        P("dp", "seq", None),
        P("dp", "seq", None),
        P(("dp", "seq"), None),
        P(("dp", "seq")),
        P(("dp", "seq"), None),
        P(("dp", "seq"), None),
        P(("dp", "seq")),
        P(("dp", "seq"), None),
        P(("dp", "seq")),
        P(("dp", "seq")),
        P(("dp", "seq")),
        P(("dp", "seq"), None),
        P(("dp", "seq")),
        P(("dp", "seq"), None),
        P(("dp", "seq")),
        P(("dp", "seq")),
        P(("dp", "seq")),
    )
    return jax.shard_map(
        per_device, mesh=mesh, in_specs=in_specs, out_specs=out_specs, check_vma=False
    )
```

profile of v0, /device:TPU:0, one launch (start us, length us, event | category | flops | bytes accessed | tf_op | source)
XLA Modules:
  0.0 1976.7 jit_solution(12275357442475884582)
XLA Ops:
  17.0 42.6 %all-reduce.19 = (bf16[3072]{0:T(1024)(128)(2,1)S(1)}, bf16[768]{0:T(1024)(128)(2,1)S(1)}, bf16[768]{0:T(1024)(128)(2,1)S(1)}, bf16[768]{0:T(1024)(128)(2,1)S(1)...) all-reduce(bf16[3072]{0:T(1024)(128)(2,1)S(1)} %dynamic-update-slic, ...), channel_id=1, replica_groups=mesh['dp'=4,'seq'=8] {'dp','seq'}, use_global_device_ids=true, to_apply=%add.1 | all-reduce | flops 11520 | bytes 46080
  59.6 8.2 all-gather.8.cloned.1.call-done
  71.1 52.4 %all-gather.10.cloned.1.call-done = bf16[768,768]{1,0:T(8,128)(2,1)} async-done(((bf16[24,768]{1,0:T(8,128)(2,1)}), bf16[768,768]{1,0:T(8,128)(2,1)}) %all-gather.10.cloned.1.call-update) | async-done | bytes 1179664 | tf_op jit(solution)/shard_map/all_gather | solution.py:177
  138.8 50.1 %all-gather.14.cloned.1.call-done = bf16[1536,1536]{1,0:T(8,128)(2,1)} async-done(((bf16[48,1536]{1,0:T(8,128)(2,1)}), bf16[1536,1536]{1,0:T(8,128)(2,1)}) %all-gather.14.cloned.1.call-update) | async-done | bytes 4718608 | tf_op jit(solution)/shard_map/all_gather | solution.py:174
  189.0 8.3 add_convert_fusion.1
  211.1 108.1 %all-gather.12.cloned.1.call-done = bf16[4,2048,1536]{1,2,0:T(8,128)(2,1)} async-done(((bf16[4,256,1536]{1,2,0:T(8,128)(2,1)}), bf16[4,2048,1536]{1,2,0:T(8,128)(2,1)}) %all-gather.12.cloned.1.call-update) | async-done | bytes 25165840 | tf_op jit(solution)/shard_map/all_gather | solution.py:242
  319.2 240.7 %while.34 = (s32[]{:T(128)}, f32[4,256,12,64]{1,3,2,0:T(8,128)}, f32[4,256,12]{1,2,0:T(8,128)S(1)}, f32[4,256,12]{1,2,0:T(8,128)S(1)}, s32[4,256]{1,0:T(4,128)S(...) while((s32[]{:T(128)}, f32[4,256,12,64]{1,3,2,0:T(8,128)}, ...), condition=%wide.region_3.4_spmd.clone, body=%wide.region_0.3_spmd.clone.sunk | while | flops 1259403264 | bytes 137130288 | solution.py:94
  570.9 36.2 %multiply_convert_fusion = (bf16[1024,3072]{1,0:T(8,128)(2,1)}, f32[1024,3072]{1,0:T(8,128)}, f32[1024,3072]{1,0:T(8,128)}) fusion(f32[3072]{0:T(1024)S(1)} %copy-done.53, bf16[768,3072]{1,0:T(8,128)(2,1)} %all-gather.18.cloned.1.call-done, f32[1024,768]{1,0:T(8,128)S(1)} %get-tuple-element.646, f32[768]{0:T(1024)S(1)} %copy-done.37, ...), kind=kOutput, calls=%fused_computation.66 | convolution fusion | flops 5043388416 | bytes 39348224 | tf_op jit(solution)/shard_map/dot_general | solution.py:26
  607.1 9.0 fusion.66
  624.0 18.7 convert_reduce_fusion
  642.8 10.1 multiply_reduce_fusion
  668.3 8.5 broadcast_in_dim.155
  676.8 398.1 %while.35 = (s32[]{:T(128)}, f32[4,256,12,128]{1,3,2,0:T(8,128)}, bf16[4,2048,1536]{1,2,0:T(8,128)(2,1)}, bf16[4,2048,1536]{1,2,0:T(8,128)(2,1)}, s32[4,2048]{1,...) while((s32[]{:T(128)}, f32[4,256,12,128]{1,3,2,0:T(8,128)}, ...), condition=%wide.region_14.15_spmd.clone, body=%wide.region_13.14_spmd.clone.sunk | while | flops 3289124864 | bytes 186581392 | solution.py:320
  694.1 7.8 fusion.145
  706.5 7.6 fusion.146
  716.1 9.2 bitcast_add_fusion.5
  742.2 7.8 fusion.145
  754.6 7.6 fusion.146
  764.2 11.0 bitcast_add_fusion.5
  792.1 7.8 fusion.145
  804.6 7.6 fusion.146
  814.2 11.0 bitcast_add_fusion.5
  842.1 7.8 fusion.145
  854.6 7.6 fusion.146
  864.1 11.0 bitcast_add_fusion.5
  892.0 7.8 fusion.145
  904.5 7.6 fusion.146
  914.0 11.0 bitcast_add_fusion.5
  941.9 7.8 fusion.145
  954.4 7.6 fusion.146
  964.0 11.0 bitcast_add_fusion.5
  991.8 7.8 fusion.145
  1013.8 11.0 bitcast_add_fusion.5
  1041.7 7.8 fusion.145
  1054.2 7.6 fusion.146
  1063.8 11.0 bitcast_add_fusion.5
  1080.1 11.8 fusion.57
  1093.7 12.1 fusion.71
  1115.6 7.9 fusion.50
  1123.6 107.3 %reduce-scatter.12.cloned.1.call-done = bf16[4,256,1536]{1,2,0:T(8,128)(2,1)} async-done(((bf16[4,2048,1536]{1,2,0:T(8,128)(2,1)}), bf16[4,256,1536]{1,2,0:T(8,128)(2,1)}) %reduce-scatter.12.cloned.1.call-update) | async-done | bytes 3145744 | tf_op jit(solution)/shard_map/reduce_scatter | solution.py:326
  1246.4 10.0 fusion.68
  1257.2 41.1 %all-reduce.18 = (f32[3072]{0:T(1024)S(1)}, f32[768]{0:T(1024)S(1)}, f32[768]{0:T(1024)S(1)}, f32[768]{0:T(1024)S(1)}, f32[768]{0:T(1024)S(1)}, /*index=5*/f32[3...) all-reduce(f32[3072]{0:T(1024)S(1)} %pad_maximum_fusion.7, ...), channel_id=4, replica_groups=mesh['dp'=4,'seq'=8] {'dp','seq'}, use_global_device_ids=true, to_apply=%region_19.20.clone | all-reduce | flops 11520 | bytes 92160
  1313.8 22.6 %reduce-scatter.16.cloned.1.call-done = f32[24,768]{1,0:T(8,128)} async-done(((f32[768,768]{1,0:T(8,128)}), f32[24,768]{1,0:T(8,128)}) %reduce-scatter.16.cloned.1.call-update) | async-done | bytes 73744 | tf_op jit(solution)/shard_map/reduce_scatter | solution.py:358
  1336.4 141.6 %reduce-scatter.18.cloned.1.call-done = f32[24,3072]{1,0:T(8,128)} async-done(((f32[768,3072]{1,0:T(8,128)}), f32[24,3072]{1,0:T(8,128)}) %reduce-scatter.18.cloned.1.call-update) | async-done | bytes 294928 | tf_op jit(solution)/shard_map/reduce_scatter | solution.py:362
  1478.0 141.7 %reduce-scatter.20.cloned.1.call-done = f32[96,768]{1,0:T(8,128)} async-done(((f32[3072,768]{1,0:T(8,128)}), f32[96,768]{1,0:T(8,128)}) %reduce-scatter.20.cloned.1.call-update) | async-done | bytes 294928 | tf_op jit(solution)/shard_map/reduce_scatter | solution.py:364
  1619.7 141.5 %reduce-scatter.14.cloned.1.call-done = f32[48,1536]{1,0:T(8,128)} async-done(((f32[1536,1536]{1,0:T(8,128)}), f32[48,1536]{1,0:T(8,128)}) %reduce-scatter.14.cloned.1.call-update) | async-done | bytes 294928 | tf_op jit(solution)/shard_map/reduce_scatter | solution.py:353
  1761.2 104.4 %reduce-scatter.24.cloned.1.call-done = f32[24,768]{1,0:T(8,128)} async-done(((f32[768,768]{1,0:T(8,128)}), f32[24,768]{1,0:T(8,128)}) %reduce-scatter.24.cloned.1.call-update) | async-done | bytes 73744
  1865.6 104.3 %reduce-scatter.22.cloned.1.call-done = f32[24,768]{1,0:T(8,128)} async-done(((f32[768,768]{1,0:T(8,128)}), f32[24,768]{1,0:T(8,128)}) %reduce-scatter.22.cloned.1.call-update) | async-done | bytes 73744
  (559 shorter events, 559.6 us)
Async XLA Ops:
  7.2 60.6 %all-gather.8.cloned.1.call-start = ((), (), s32[]{:S(2)}) async-start(), calls=%async_computation.7 | async-start | bytes 1216512 | tf_op jit(solution)/shard_map/all_gather | solution.py:176
  7.9 115.6 %all-gather.10.cloned.1.call-start = ((), (), s32[]{:S(2)}) async-start(), calls=%async_computation.8 | async-start | bytes 1216512 | tf_op jit(solution)/shard_map/all_gather | solution.py:177
  8.7 180.3 %all-gather.14.cloned.1.call-start = ((), (), s32[]{:S(2)}) async-start(), calls=%async_computation.10 | async-start | bytes 4866048 | tf_op jit(solution)/shard_map/all_gather | solution.py:174
  9.4 309.8 %all-gather.12.cloned.1.call-start = ((), (), s32[]{:S(2)}) async-start(), calls=%async_computation.9 | async-start | bytes 28311552 | tf_op jit(solution)/shard_map/all_gather | solution.py:242
  67.8 55.7 %copy-start.20 = (bf16[4,256,768]{2,1,0:T(8,128)(2,1)S(1)}, bf16[4,256,768]{2,1,0:T(8,128)(2,1)}, u32[]{:S(2)}) copy-start(bf16[4,256,768]{2,1,0:T(8,128)(2,1)} %param.23) | copy-start | bytes 4718596
  128.5 437.8 %all-gather.16.cloned.1.call-start = ((), (), s32[]{:S(2)}) async-start(), calls=%async_computation.11 | async-start | bytes 1216512 | tf_op jit(solution)/shard_map/all_gather | solution.py:179
  129.0 441.7 %all-gather.18.cloned.1.call-start = ((), (), s32[]{:S(2)}) async-start(), calls=%async_computation.12 | async-start | bytes 4866048 | tf_op jit(solution)/shard_map/all_gather | solution.py:183
  129.6 477.4 %all-gather.20.cloned.1.call-start = ((), (), s32[]{:S(2)}) async-start(), calls=%async_computation.13 | async-start | bytes 4866048 | tf_op jit(solution)/shard_map/all_gather | solution.py:185
  130.4 1100.5 %reduce-scatter.12.cloned.1.call-start = ((), (), s32[]{:S(2)}) async-start(), calls=%async_computation.14 | async-start | bytes 28311552 | tf_op jit(solution)/shard_map/reduce_scatter | solution.py:326
  131.9 57.1 %copy-start.41 = (f32[4,256]{1,0:T(4,128)}, f32[4,256]{1,0:T(4,128)S(1)}, u32[]{:S(2)}) copy-start(f32[4,256]{1,0:T(4,128)S(1)} %get-tuple-element.621) | copy-start | bytes 12292
  131.9 65.4 %copy-start.39 = (f32[1,2,4,128]{3,1,2,0:T(2,128)}, f32[1,2,4,128]{3,1,2,0:T(2,128)S(1)}, u32[]{:S(2)}) copy-start(f32[1,2,4,128]{3,1,2,0:T(2,128)S(1)} %copy.107) | copy-start | bytes 12292
  131.9 65.4 %copy-start.51 = (f32[1024]{0:T(1024)}, f32[1024]{0:T(1024)S(1)}, u32[]{:S(2)}) copy-start(f32[1024]{0:T(1024)S(1)} %get-tuple-element.644) | copy-start | bytes 12292
  328.7 13.3 copy-start.4
  335.0 8.2 copy-start.3
  357.3 13.5 copy-start.4
  363.8 8.3 copy-start.3
  387.6 13.4 copy-start.4
  393.9 8.2 copy-start.3
  417.7 13.6 copy-start.4
  424.3 8.4 copy-start.3
  448.3 13.3 copy-start.4
  454.6 8.3 copy-start.3
  478.3 14.0 copy-start.4
  484.6 8.9 copy-start.3
  509.0 13.3 copy-start.4
  515.4 8.2 copy-start.3
  539.0 13.3 copy-start.4
  545.4 8.2 copy-start.3
  570.1 82.8 %copy-start.6 = (f32[1024,768]{1,0:T(8,128)}, f32[1024,768]{1,0:T(8,128)S(1)}, u32[]{:S(2)}) copy-start(f32[1024,768]{1,0:T(8,128)S(1)} %get-tuple-element.646) | copy-start | bytes 9437188
  570.1 82.8 %copy-start.31 = (f32[1024]{0:T(1024)}, f32[1024]{0:T(1024)S(1)}, u32[]{:S(2)}) copy-start(f32[1024]{0:T(1024)S(1)} %broadcast_multiply_fusion.7) | copy-start | bytes 12292
  570.6 82.3 %copy-start.33 = (f32[1024]{0:T(1024)}, f32[1024]{0:T(1024)S(1)}, u32[]{:S(2)}) copy-start(f32[1024]{0:T(1024)S(1)} %fusion.51) | copy-start | bytes 12292
  570.7 36.4 %copy-start.55 = (f32[768]{0:T(1024)S(1)}, f32[768]{0:T(1024)}, u32[]{:S(2)}) copy-start(f32[768]{0:T(1024)} %convert_element_type.226) | copy-start | bytes 9220
  668.2 8.5 copy-start.28
  686.7 7.3 copy-start.18
  734.8 7.3 copy-start.18
  784.8 7.3 copy-start.18
  834.8 7.3 copy-start.18
  884.7 7.3 copy-start.18
  934.6 7.3 copy-start.18
  984.5 7.3 copy-start.18
  1075.0 261.4 %reduce-scatter.16.cloned.1.call-start = ((), (), s32[]{:S(2)}) async-start(), calls=%async_computation.16 | async-start | bytes 2433024 | tf_op jit(solution)/shard_map/reduce_scatter | solution.py:358
  1080.0 398.1 %reduce-scatter.18.cloned.1.call-start = ((), (), s32[]{:S(2)}) async-start(), calls=%async_computation.17 | async-start | bytes 9732096 | tf_op jit(solution)/shard_map/reduce_scatter | solution.py:362
  1091.9 527.8 %reduce-scatter.20.cloned.1.call-start = ((), (), s32[]{:S(2)}) async-start(), calls=%async_computation.18 | async-start | bytes 9732096 | tf_op jit(solution)/shard_map/reduce_scatter | solution.py:364
  1105.8 655.4 %reduce-scatter.14.cloned.1.call-start = ((), (), s32[]{:S(2)}) async-start(), calls=%async_computation.15 | async-start | bytes 9732096 | tf_op jit(solution)/shard_map/reduce_scatter | solution.py:353
  1123.5 109.1 %copy-start.21 = (bf16[4,256,768]{2,1,0:T(8,128)(2,1)S(1)}, bf16[4,256,768]{2,1,0:T(8,128)(2,1)}, u32[]{:S(2)}) copy-start(bf16[4,256,768]{2,1,0:T(8,128)(2,1)} %param.23) | copy-start | bytes 4718596
  1123.5 742.1 %reduce-scatter.24.cloned.1.call-start = ((), (), s32[]{:S(2)}) async-start(), calls=%async_computation.20 | async-start | bytes 2433024
  1238.5 731.4 %reduce-scatter.22.cloned.1.call-start = ((), (), s32[]{:S(2)}) async-start(), calls=%async_computation.19 | async-start | bytes 2433024
  1257.2 46.4 %slice-start = ((bf16[4,256,1536]{1,2,0:T(8,128)(2,1)}), bf16[4,256,768]{1,2,0:T(8,128)(2,1)S(1)}, s32[]{:S(2)}) async-start(bf16[4,256,1536]{1,2,0:T(8,128)(2,1)} %reduce-scatter.12.cloned.1.call-done), calls=%async_computation.21 | async-start | bytes 3145728 | tf_op jit(solution)/shard_map/slice | solution.py:330
  (90 other events, 307.3 us)
Sparse Core Ops, SparseCore 0:
  10.9 56.8 all-gather.7
  70.7 52.7 all-gather.9
  126.4 62.4 all-gather.13
  190.7 128.4 all-gather.11
  321.9 53.9 all-gather.15
  378.7 62.4 all-gather.17
  444.1 61.9 all-gather.19
  1075.1 155.8 reduce-scatter.11
  1236.8 99.6 reduce-scatter.15
  1342.8 135.2 reduce-scatter.17
  1484.5 135.1 reduce-scatter.19
  1626.0 135.0 reduce-scatter.13
  1767.0 98.5 reduce-scatter.23
  1871.3 98.5 reduce-scatter.21
where the time goes:
time: 1990 us; the launch traced here: 1980 us
  waiting for transfers between devices  986 us (50%)
  matrix products  531 us (27%)
  local copies, waits for them, and re-layouts  200 us (10%)
  other arithmetic  158 us (8%)
  blocking collectives  83.7 us (4%)
    unnamed x16, waiting for transfers between devices  213 us
    reduce_scatter x1, waiting for transfers between devices, per_device(): lax.psum_scatter(grad_down, ('dp', 'seq'), scatter_dimension=0, tiled=True)  142 us
    reduce_scatter x1, waiting for transfers between devices, per_device(): lax.psum_scatter(grad_up, ('dp', 'seq'), scatter_dimension=0, tiled=True)  142 us
    reduce_scatter x1, waiting for transfers between devices, per_device(): lax.psum_scatter(grad_query, ('dp', 'seq'), scatter_dimension=0, tiled=True)  141 us
    all_gather x1, waiting for transfers between devices, per_device(): lax.all_gather(local_kv, 'seq', axis=1, tiled=True)  108 us
    reduce_scatter x1, waiting for transfers between devices, per_device(): lax.psum_scatter(grad_kv_all.astype(jnp.bfloat16), 'seq', scatter_dimensi...  107 us
    dot_general x16, matrix products, block_scores(): jnp.einsum('sqhc,skhc->sqhk', queries, joined, preferred_element_type=jnp...  102 us
    dot_general x8, matrix products, back_block(): jnp.einsum('sqhk,skhc->sqhc', grad_raw, joined, preferred_element_type=jn...  86.2 us
  transfers between devices with their start and end apart: 14, of which 11 were waited for; matrix products, arithmetic and copies ran while one was open for 21% of the time, Pallas kernels for 0%

commit v1 on v0

v1 whole, which is shorter than its diff:
```python
import functools
import math

import jax
import jax.numpy as jnp
from jax import lax
from jax.experimental import pallas as pl
from jax.experimental.pallas import tpu as pltpu
from jax.sharding import Mesh
from jax.sharding import PartitionSpec as P

HEAD_DIM = 64
DOCS = 8
NORM_EPS = 1e-12
FAR = 2.0**50
LOWEST = -3.0e38
LANES = 128
BF16 = jnp.bfloat16
F32 = jnp.float32


def params(*semantics):
    return pltpu.CompilerParams(
        dimension_semantics=semantics, vmem_limit_bytes=60 * 1024 * 1024
    )


def dot_nn(a, b):
    return lax.dot_general(a, b, (((1,), (0,)), ((), ())), preferred_element_type=F32)


def dot_nt(a, b):
    return lax.dot_general(a, b, (((1,), (1,)), ((), ())), preferred_element_type=F32)


def dot_tn(a, b):
    return lax.dot_general(a, b, (((0,), (0,)), ((), ())), preferred_element_type=F32)


def whole(shape):
    zeros = (0,) * len(shape)
    return pl.BlockSpec(shape, lambda *_: zeros, pipeline_mode=pl.Buffered(1))


def rel_start(me, step, parts, size):
    return pl.multiple_of(lax.rem(me + step, parts) * size, size)


def proj_body(parts, own, heads, me_ref, *refs):
    x_refs = refs[:parts]
    kc_ref, kr_ref, wq_ref, wk_ref, wv_ref, bq_ref, bv_ref = refs[parts : parts + 7]
    q_ref, kj_ref, kjt_ref, vx_ref, vt_ref = refs[parts + 7 :]
    me = me_ref[0]
    width = x_refs[0].shape[1]
    for step in range(parts):
        at = rel_start(me, step, parts, own)
        rows = pl.ds(at, own)
        x = x_refs[step][...]
        entity = kc_ref[rows, :] > 0.5
        word_q = dot_nn(x, wq_ref[:width, :]) + bq_ref[0:1, :]
        entity_q = dot_nn(x, wq_ref[width:, :]) + bq_ref[1:2, :]
        queries = jnp.where(entity, entity_q, word_q).astype(BF16)
        q_ref[rows, :] = queries * BF16(1.0 / math.sqrt(HEAD_DIM))
        keys = dot_nn(x, wk_ref[...]).astype(BF16).astype(F32)
        values = (dot_nn(x, wv_ref[...]) + bv_ref[...]).astype(BF16).astype(F32)
        keys_t = keys.T
        values_t = values.T
        row_entity = kr_ref[:, rows] > 0.5
        zero = jnp.zeros((own, HEAD_DIM), F32)
        for head in range(heads):
            part = slice(head * HEAD_DIM, (head + 1) * HEAD_DIM)
            wide = slice(head * LANES, (head + 1) * LANES)
            k = keys[:, part]
            kj_ref[rows, wide] = jnp.concatenate(
                [jnp.where(entity, 0.0, k), jnp.where(entity, k, 0.0)], axis=1
            ).astype(BF16)
            kt = keys_t[part, :]
            kjt_ref[wide, rows] = jnp.concatenate(
                [jnp.where(row_entity, 0.0, kt), jnp.where(row_entity, kt, 0.0)], axis=0
            ).astype(BF16)
            v = values[:, part]
            pair = [v, zero] if head % 2 == 0 else [zero, v]
            vx_ref[rows, wide] = jnp.concatenate(pair, axis=1).astype(BF16)
        vt_ref[:, rows] = values_t.astype(BF16)


def project(me, xs, kind_col, kind_row, wq, wk, wv, bq, bv, groups, own, heads):
    parts = len(xs)
    rows = parts * own
    length = groups * rows
    width = xs[0].shape[1]
    feats = heads * HEAD_DIM
    grid_spec = pltpu.PrefetchScalarGridSpec(
        num_scalar_prefetch=1,
        grid=(groups,),
        in_specs=[pl.BlockSpec((own, width), lambda i, m: (i, 0))] * parts
        + [
            pl.BlockSpec((rows, 1), lambda i, m: (i, 0)),
            pl.BlockSpec((1, rows), lambda i, m: (0, i)),
            whole(wq.shape),
            whole(wk.shape),
            whole(wv.shape),
            whole(bq.shape),
            whole(bv.shape),
        ],
        out_specs=[
            pl.BlockSpec((rows, 2 * feats), lambda i, m: (i, 0)),
            pl.BlockSpec((rows, 2 * feats), lambda i, m: (i, 0)),
            pl.BlockSpec((2 * feats, rows), lambda i, m: (0, i)),
            pl.BlockSpec((rows, 2 * feats), lambda i, m: (i, 0)),
            pl.BlockSpec((feats, rows), lambda i, m: (0, i)),
        ],
    )
    return pl.pallas_call(
        functools.partial(proj_body, parts, own, heads),
        grid_spec=grid_spec,
        out_shape=[
            jax.ShapeDtypeStruct((length, 2 * feats), BF16),
            jax.ShapeDtypeStruct((length, 2 * feats), BF16),
            jax.ShapeDtypeStruct((2 * feats, length), BF16),
            jax.ShapeDtypeStruct((length, 2 * feats), BF16),
            jax.ShapeDtypeStruct((feats, length), BF16),
        ],
        compiler_params=params("arbitrary"),
        name="project",
    )(me, *xs, kind_col, kind_row, wq, wk, wv, bq, bv)


def attend_body(parts, own, heads, me_ref, lo_ref, hi_ref, *refs):
    q_ref, mq_ref, kj_ref, mk_ref, vt_ref = refs[:5]
    out_refs = refs[5 : 5 + parts]
    lse_ref, acc_ref, max_ref, sum_ref = refs[5 + parts :]
    me = me_ref[0]
    group = pl.program_id(0)
    for step in range(parts):
        at = rel_start(me, step, parts, own)
        rows = pl.ds(at, own)
        block = group * parts + lax.rem(me + step, parts)
        acc_ref[...] = jnp.zeros_like(acc_ref)
        max_ref[...] = jnp.full_like(max_ref, LOWEST)
        sum_ref[...] = jnp.zeros_like(sum_ref)

        def fold(kb, carry):
            keys_at = pl.ds(pl.multiple_of(kb * own, own), own)
            key_mark = mk_ref[keys_at, :]
            query_mark = mq_ref[rows, :]
            for head in range(heads):
                wide = slice(head * LANES, (head + 1) * LANES)
                part = slice(head * HEAD_DIM, (head + 1) * HEAD_DIM)
                k = jnp.concatenate([kj_ref[keys_at, wide], key_mark], axis=1)
                q = jnp.concatenate([q_ref[rows, wide], query_mark], axis=1)
                scores = dot_nt(k, q)
                old_max = max_ref[head : head + 1, :]
                new_max = jnp.maximum(old_max, jnp.max(scores, axis=0, keepdims=True))
                factor = jnp.exp(old_max - new_max)
                terms = jnp.exp(scores - new_max)
                sum_ref[head : head + 1, :] = sum_ref[head : head + 1, :] * factor + jnp.sum(
                    terms, axis=0, keepdims=True
                )
                acc_ref[part, :] = acc_ref[part, :] * factor + dot_nn(
                    vt_ref[part, keys_at], terms.astype(BF16)
                )
                max_ref[head : head + 1, :] = new_max
            return carry

        lax.fori_loop(lo_ref[block], hi_ref[block], fold, 0)
        lse_ref[:, rows] = max_ref[...] + jnp.log(sum_ref[...])
        inverse = 1.0 / sum_ref[...]
        for first in range(0, heads, 2):
            last = min(first + 2, heads)
            tall = jnp.concatenate(
                [
                    acc_ref[h * HEAD_DIM : (h + 1) * HEAD_DIM, :] * inverse[h : h + 1, :]
                    for h in range(first, last)
                ],
                axis=0,
            )
            out_refs[step][:, first * HEAD_DIM : last * HEAD_DIM] = tall.T.astype(BF16)


def attend(me, lo, hi, q, mq, kj, mk, vt, groups, parts, own, heads):
    rows = parts * own
    length = groups * rows
    feats = heads * HEAD_DIM
    stats = 8 * ((heads + 7) // 8)
    grid_spec = pltpu.PrefetchScalarGridSpec(
        num_scalar_prefetch=3,
        grid=(groups,),
        in_specs=[
            pl.BlockSpec((rows, 2 * feats), lambda i, *_: (i, 0)),
            pl.BlockSpec((rows, LANES), lambda i, *_: (i, 0)),
            whole(kj.shape),
            whole(mk.shape),
            whole(vt.shape),
        ],
        out_specs=[pl.BlockSpec((own, feats), lambda i, *_: (i, 0))] * parts
        + [pl.BlockSpec((stats, rows), lambda i, *_: (0, i))],
        scratch_shapes=[
            pltpu.VMEM((feats, own), F32),
            pltpu.VMEM((stats, own), F32),
            pltpu.VMEM((stats, own), F32),
        ],
    )
    outs = pl.pallas_call(
        functools.partial(attend_body, parts, own, heads),
        grid_spec=grid_spec,
        out_shape=[jax.ShapeDtypeStruct((groups * own, feats), BF16)] * parts
        + [jax.ShapeDtypeStruct((stats, length), F32)],
        compiler_params=params("arbitrary"),
        name="attend",
    )(me, lo, hi, q, mq, kj, mk, vt)
    return outs[:parts], outs[parts]


def attend_back_body(parts, own, heads, groups, me_ref, lo_ref, hi_ref, *refs):
    q_ref, mq_ref, kj_ref, kjt_ref, vx_ref, mk_ref, kc_ref, lse_ref = refs[:8]
    grad_refs = refs[8 : 8 + parts]
    out_refs = refs[8 + parts : 8 + 2 * parts]
    dq_ref, dk_ref, dv_ref = refs[8 + 2 * parts : 11 + 2 * parts]
    grad_nat, delta_ref, dqt_ref, dk_acc, dv_acc = refs[11 + 2 * parts :]
    me = me_ref[0]
    kb = pl.program_id(0)
    feats = heads * HEAD_DIM
    pairs = (heads + 1) // 2
    stats = delta_ref.shape[0]

    @pl.when(kb == 0)
    def _():
        dqt_ref[...] = jnp.zeros_like(dqt_ref)
        if feats != grad_nat.shape[1]:
            grad_nat[...] = jnp.zeros_like(grad_nat)
        head_row = lax.broadcasted_iota(jnp.int32, (stats, feats), 0)
        head_col = lax.broadcasted_iota(jnp.int32, (stats, feats), 1) // HEAD_DIM
        pick = (head_row == head_col).astype(F32)

        def take(group, carry):
            for step in range(parts):
                source = pl.ds(pl.multiple_of(group * own, own), own)
                at = pl.multiple_of((group * parts + lax.rem(me + step, parts)) * own, own)
                grad = grad_refs[step][source, :]
                grad_nat[pl.ds(at, own), :feats] = grad
                product = grad.astype(F32) * out_refs[step][source, :].astype(F32)
                delta_ref[:, pl.ds(at, own)] = lax.dot_general(
                    pick,
                    product,
                    (((1,), (1,)), ((), ())),
                    precision=lax.Precision.HIGHEST,
                    preferred_element_type=F32,
                )
            return carry

        lax.fori_loop(0, groups, take, 0)

    dk_acc[...] = jnp.zeros_like(dk_acc)
    dv_acc[...] = jnp.zeros_like(dv_acc)
    key_mark = mk_ref[...]

    def fold(qb, carry):
        rows = pl.ds(pl.multiple_of(qb * own, own), own)
        query_mark = mq_ref[rows, :]
        for head in range(heads):
            wide = slice(head * LANES, (head + 1) * LANES)
            pair = slice((head // 2) * LANES, (head // 2 + 1) * LANES)
            query = q_ref[rows, wide]
            k = jnp.concatenate([kj_ref[:, wide], key_mark], axis=1)
            q = jnp.concatenate([query, query_mark], axis=1)
            probs = jnp.exp(dot_nt(k, q) - lse_ref[head : head + 1, rows])
            grad = grad_nat[rows, pair]
            grad_probs = dot_nt(vx_ref[:, wide], grad)
            grad_raw = (probs * (grad_probs - delta_ref[head : head + 1, rows])).astype(BF16)
            dv_acc[:, wide] += dot_nn(probs.astype(BF16), grad)
            dk_acc[:, wide] += dot_nn(grad_raw, query)
            dqt_ref[wide, rows] += dot_nn(kjt_ref[wide, :], grad_raw)
        return carry

    lax.fori_loop(lo_ref[kb], hi_ref[kb], fold, 0)

    entity = kc_ref[...] > 0.5
    for first in range(0, heads, 2):
        grads_k = []
        grads_v = []
        for head in range(first, min(first + 2, heads)):
            base = head * LANES
            word_half = dk_acc[:, base : base + HEAD_DIM]
            entity_half = dk_acc[:, base + HEAD_DIM : base + LANES]
            grads_k.append(jnp.where(entity, entity_half, word_half))
            shift = (head % 2) * HEAD_DIM
            grads_v.append(dv_acc[:, base + shift : base + shift + HEAD_DIM])
        cols = slice(first * HEAD_DIM, first * HEAD_DIM + len(grads_k) * HEAD_DIM)
        dk_ref[:, cols] = jnp.concatenate(grads_k, axis=1).astype(BF16)
        dv_ref[:, cols] = jnp.concatenate(grads_v, axis=1).astype(BF16)

    @pl.when(kb == pl.num_programs(0) - 1)
    def _():
        def turn(qb, carry):
            rows = pl.ds(pl.multiple_of(qb * own, own), own)
            for head in range(heads):
                wide = slice(head * LANES, (head + 1) * LANES)
                tall = dqt_ref[wide, rows] * (1.0 / math.sqrt(HEAD_DIM))
                dq_ref[rows, wide] = tall.T.astype(BF16)
            return carry

        lax.fori_loop(0, pl.num_programs(0), turn, 0)


def attend_back(me, lo, hi, q, mq, kj, kjt, vx, mk, kind_col, lse, grads, outs, own, heads):
    parts = len(grads)
    length = q.shape[0]
    blocks = length // own
    feats = heads * HEAD_DIM
    pairs = (heads + 1) // 2
    stats = lse.shape[0]
    grid_spec = pltpu.PrefetchScalarGridSpec(
        num_scalar_prefetch=3,
        grid=(blocks,),
        in_specs=[
            whole(q.shape),
            whole(mq.shape),
            pl.BlockSpec((own, 2 * feats), lambda i, *_: (i, 0)),
            pl.BlockSpec((2 * feats, own), lambda i, *_: (0, i)),
            pl.BlockSpec((own, 2 * feats), lambda i, *_: (i, 0)),
            pl.BlockSpec((own, LANES), lambda i, *_: (i, 0)),
            pl.BlockSpec((own, 1), lambda i, *_: (i, 0)),
            whole(lse.shape),
        ]
        + [whole(g.shape) for g in grads]
        + [whole(o.shape) for o in outs],
        out_specs=[
            whole(q.shape),
            pl.BlockSpec((own, feats), lambda i, *_: (i, 0)),
            pl.BlockSpec((own, feats), lambda i, *_: (i, 0)),
        ],
        scratch_shapes=[
            pltpu.VMEM((length, pairs * LANES), BF16),
            pltpu.VMEM((stats, length), F32),
            pltpu.VMEM((2 * feats, length), F32),
            pltpu.VMEM((own, 2 * feats), F32),
            pltpu.VMEM((own, 2 * feats), F32),
        ],
    )
    return pl.pallas_call(
        functools.partial(attend_back_body, parts, own, heads, blocks // parts),
        grid_spec=grid_spec,
        out_shape=[
            jax.ShapeDtypeStruct(q.shape, BF16),
            jax.ShapeDtypeStruct((length, feats), BF16),
            jax.ShapeDtypeStruct((length, feats), BF16),
        ],
        compiler_params=params("arbitrary"),
        name="attend_back",
    )(me, lo, hi, q, mq, kj, kjt, vx, mk, kind_col, lse, *grads, *outs)


def norm_stats(value):
    center = value - jnp.mean(value, axis=1, keepdims=True)
    scale = lax.rsqrt(jnp.mean(center * center, axis=1, keepdims=True) + NORM_EPS)
    return center * scale, scale


def norm_back(xhat, scale, grad):
    mean_one = jnp.mean(grad, axis=1, keepdims=True)
    mean_two = jnp.mean(grad * xhat, axis=1, keepdims=True)
    return scale * (grad - mean_one - xhat * mean_two)


def feed_body(parts, feats, me_ref, *refs):
    att_refs = refs[:parts]
    x_ref, ct_ref, wo_ref, wu_ref, wd_ref, bu_ref, vec_ref = refs[parts : parts + 7]
    outs = refs[parts + 7 :]
    out_ref, gf_ref, nat_ref, act_ref, gup_ref, low_ref, g2_ref, g1_ref = outs[:8]
    gatt_refs = outs[8 : 8 + parts]
    su_ref, sv_ref, deriv_ref = outs[8 + parts :]
    me = me_ref[0]
    ff = wu_ref.shape[1]
    chunk = min(768, ff)

    @pl.when(pl.program_id(0) == 0)
    def _():
        su_ref[...] = jnp.zeros_like(su_ref)
        sv_ref[...] = jnp.zeros_like(sv_ref)

    bias_out, gain_one, shift_one = vec_ref[0:1, :], vec_ref[1:2, :], vec_ref[2:3, :]
    bias_down, gain_two, shift_two = vec_ref[3:4, :], vec_ref[4:5, :], vec_ref[5:6, :]
    first_sum = x_ref[...].astype(F32) + bias_out
    for step in range(parts):
        at = rel_start(me, step, parts, feats)
        att = att_refs[step][...]
        for own in range(parts):

            @pl.when(lax.rem(me + step, parts) == own)
            def _(att=att, own=own):
                nat_ref[:, own * feats : (own + 1) * feats] = att

        first_sum = first_sum + dot_nn(att, wo_ref[pl.ds(at, feats), :])
    hat_one, scale_one = norm_stats(first_sum)
    normed = hat_one * gain_one + shift_one
    normed_low = normed.astype(BF16)
    low_ref[...] = normed_low
    second_sum = normed + bias_down
    for at in range(0, ff, chunk):
        cols = slice(at, at + chunk)
        up = dot_nn(normed_low, wu_ref[:, cols]) + bu_ref[:, cols]
        below = 0.5 + 0.5 * lax.erf(up * math.sqrt(0.5))
        density = jnp.exp(-0.5 * up * up) * (1.0 / math.sqrt(2.0 * math.pi))
        deriv_ref[:, cols] = below + up * density
        activated = (up * below).astype(BF16)
        act_ref[:, cols] = activated
        second_sum = second_sum + dot_nn(activated, wd_ref[cols, :])
    hat_two, scale_two = norm_stats(second_sum)
    out_ref[...] = (hat_two * gain_two + shift_two).astype(BF16)
    cotangent = ct_ref[...].astype(F32)
    grad_second = norm_back(hat_two, scale_two, cotangent * gain_two)
    branch_two = grad_second.astype(BF16)
    g2_ref[...] = branch_two
    grad_normed = grad_second
    for at in range(0, ff, chunk):
        cols = slice(at, at + chunk)
        grad_up = (dot_nt(branch_two, wd_ref[cols, :]) * deriv_ref[:, cols]).astype(BF16)
        gup_ref[:, cols] = grad_up
        su_ref[:, cols] += jnp.sum(grad_up.astype(F32), axis=0, keepdims=True)
        grad_normed = grad_normed + dot_nt(grad_up, wu_ref[:, cols])
    grad_first = norm_back(hat_one, scale_one, grad_normed * gain_one)
    gf_ref[...] = grad_first
    branch_one = grad_first.astype(BF16)
    g1_ref[...] = branch_one
    for step in range(parts):
        at = rel_start(me, step, parts, feats)
        gatt_refs[step][...] = dot_nt(branch_one, wo_ref[pl.ds(at, feats), :]).astype(BF16)
    sums = (
        branch_one.astype(F32),
        grad_normed * hat_one,
        grad_normed,
        branch_two.astype(F32),
        cotangent * hat_two,
        cotangent,
    )
    for row, value in enumerate(sums):
        sv_ref[row : row + 1, :] += jnp.sum(value, axis=0, keepdims=True)


def feed(me, atts, x, ct, wo, wu, wd, bias_up, vecs, block):
    parts = len(atts)
    feats = atts[0].shape[1]
    tokens, width = x.shape
    ff = wu.shape[1]
    row = lambda cols: pl.BlockSpec((block, cols), lambda i, m: (i, 0))
    grid_spec = pltpu.PrefetchScalarGridSpec(
        num_scalar_prefetch=1,
        grid=(tokens // block,),
        in_specs=[row(feats)] * parts
        + [row(width), row(width)]
        + [whole(wo.shape), whole(wu.shape), whole(wd.shape), whole(bias_up.shape)]
        + [whole(vecs.shape)],
        out_specs=[row(width), row(width), row(width), row(ff), row(ff)]
        + [row(width), row(width), row(width)]
        + [row(feats)] * parts
        + [whole((1, ff)), whole((8, width))],
        scratch_shapes=[pltpu.VMEM((block, ff), F32)],
    )
    low = lambda cols: jax.ShapeDtypeStruct((tokens, cols), BF16)
    outs = pl.pallas_call(
        functools.partial(feed_body, parts, feats),
        grid_spec=grid_spec,
        out_shape=[
            low(width),
            jax.ShapeDtypeStruct((tokens, width), F32),
            low(width),
            low(ff),
            low(ff),
            low(width),
            low(width),
            low(width),
        ]
        + [low(feats)] * parts
        + [jax.ShapeDtypeStruct((1, ff), F32), jax.ShapeDtypeStruct((8, width), F32)],
        compiler_params=params("arbitrary"),
        name="feed",
    )(me, *atts, x, ct, wo, wu, wd, bias_up, vecs)
    return outs[:8], outs[8 : 8 + parts], outs[8 + parts], outs[9 + parts]


def unproj_body(parts, own, me_ref, *refs):
    x_refs = refs[:parts]
    kc_ref, dq_ref, dk_ref, dv_ref, gf_ref, wq_ref, wk_ref, wv_ref = refs[parts : parts + 8]
    dx_refs = refs[parts + 8 : 2 * parts + 8]
    gq_ref, gk_ref, gv_ref, sq_ref, sv_ref = refs[2 * parts + 8 :]
    me = me_ref[0]
    width = x_refs[0].shape[1]

    @pl.when(pl.program_id(0) == 0)
    def _():
        for ref in (gq_ref, gk_ref, gv_ref, sq_ref, sv_ref):
            ref[...] = jnp.zeros_like(ref)

    for step in range(parts):
        at = rel_start(me, step, parts, own)
        rows = pl.ds(at, own)
        x = x_refs[step][...]
        entity = kc_ref[rows, :] > 0.5
        dq = dq_ref[rows, :]
        dk = dk_ref[rows, :]
        dv = dv_ref[rows, :]
        dq_word = jnp.where(entity, BF16(0), dq)
        dq_entity = jnp.where(entity, dq, BF16(0))
        gq_ref[:width, :] += dot_tn(x, dq_word)
        gq_ref[width:, :] += dot_tn(x, dq_entity)
        gk_ref[...] += dot_tn(x, dk)
        gv_ref[...] += dot_tn(x, dv)
        sq_ref[0:1, :] += jnp.sum(dq_word.astype(F32), axis=0, keepdims=True)
        sq_ref[1:2, :] += jnp.sum(dq_entity.astype(F32), axis=0, keepdims=True)
        sv_ref[...] += jnp.sum(dv.astype(F32), axis=0, keepdims=True)
        dx = (
            dot_nt(dq_word, wq_ref[:width, :])
            + dot_nt(dq_entity, wq_ref[width:, :])
            + dot_nt(dk, wk_ref[...])
            + dot_nt(dv, wv_ref[...])
        )
        if step == 0:
            dx = dx + gf_ref[...]
        dx_refs[step][...] = dx.astype(dx_refs[step].dtype)


def unproject(me, xs, kind_col, dq, dk, dv, gf, wq, wk, wv, groups, own):
    parts = len(xs)
    rows = parts * own
    width = xs[0].shape[1]
    feats = dk.shape[1]
    grid_spec = pltpu.PrefetchScalarGridSpec(
        num_scalar_prefetch=1,
        grid=(groups,),
        in_specs=[pl.BlockSpec((own, width), lambda i, m: (i, 0))] * parts
        + [
            pl.BlockSpec((rows, 1), lambda i, m: (i, 0)),
            pl.BlockSpec((rows, 2 * feats), lambda i, m: (i, 0)),
            pl.BlockSpec((rows, feats), lambda i, m: (i, 0)),
            pl.BlockSpec((rows, feats), lambda i, m: (i, 0)),
            pl.BlockSpec((own, width), lambda i, m: (i, 0)),
            whole(wq.shape),
            whole(wk.shape),
            whole(wv.shape),
        ],
        out_specs=[pl.BlockSpec((own, width), lambda i, m: (i, 0))] * parts
        + [
            whole(wq.shape),
            whole(wk.shape),
            whole(wv.shape),
            whole((2, 2 * feats)),
            whole((1, feats)),
        ],
    )
    outs = pl.pallas_call(
        functools.partial(unproj_body, parts, own),
        grid_spec=grid_spec,
        out_shape=[jax.ShapeDtypeStruct((groups * own, width), F32)]
        + [jax.ShapeDtypeStruct((groups * own, width), BF16)] * (parts - 1)
        + [
            jax.ShapeDtypeStruct(wq.shape, F32),
            jax.ShapeDtypeStruct(wk.shape, F32),
            jax.ShapeDtypeStruct(wv.shape, F32),
            jax.ShapeDtypeStruct((2, 2 * feats), F32),
            jax.ShapeDtypeStruct((1, feats), F32),
        ],
        compiler_params=params("arbitrary"),
        name="unproject",
    )(me, *xs, kind_col, dq, dk, dv, gf, wq, wk, wv)
    return outs[:parts], outs[parts:]


def from_peer(value, step, parts):
    return lax.ppermute(value, "hg", [((i + step) % parts, i) for i in range(parts)])


def split_cols(shard, width):
    return jnp.concatenate(
        [shard[:, at : at + width] for at in range(0, shard.shape[1], width)], axis=0
    )


def join_cols(gathered, rows, blocks):
    devices, _, width = gathered.shape
    return (
        gathered.reshape(devices, blocks, rows, width)
        .transpose(0, 2, 1, 3)
        .reshape(devices * rows, blocks * width)
    )


def per_device(
    tokens,
    token_types,
    segment_ids,
    query_weight,
    query_bias,
    key_weight,
    value_weight,
    value_bias,
    out_weight,
    out_bias,
    norm1_gain,
    norm1_bias,
    up_weight,
    up_bias,
    down_weight,
    down_bias,
    norm2_gain,
    norm2_bias,
    cotangent,
    *,
    devices,
    parts,
):
    groups, own, width = tokens.shape
    length = segment_ids.shape[1]
    all_heads = width // HEAD_DIM
    heads = all_heads // parts
    feats = heads * HEAD_DIM
    ff = up_weight.shape[1]
    everyone = ("dp", "grp", "hg")
    me = lax.axis_index("hg")
    mine = lax.axis_index("grp")
    me_arr = me.reshape(1).astype(jnp.int32)

    q_rows, k_rows = query_weight.shape[0], key_weight.shape[0]
    u_rows, d_rows = up_weight.shape[0], down_weight.shape[0]
    q_blocks, u_blocks = query_weight.shape[1] // width, ff // width
    pack = jnp.concatenate(
        [
            split_cols(query_weight, width),
            key_weight,
            value_weight,
            out_weight,
            split_cols(up_weight, width),
            down_weight,
        ],
        axis=0,
    )
    bundle = lax.all_gather(pack, everyone, axis=0, tiled=False)
    vec_pack = jnp.concatenate(
        [out_bias, norm1_gain, norm1_bias, down_bias, norm2_gain, norm2_bias, value_bias]
        + [query_bias, up_bias]
    ).reshape(1, -1)
    vec_all = lax.all_gather(vec_pack, everyone, axis=0, tiled=True).astype(F32)

    to_groups = lambda v: lax.all_to_all(v, "grp", 0, 0, tiled=True)
    x_mine = to_groups(tokens).reshape(groups * own, width)
    xs = [x_mine] + [from_peer(x_mine, step, parts) for step in range(1, parts)]
    ct = to_groups(cotangent).reshape(groups * own, width)
    kinds = lax.dynamic_index_in_dim(token_types, mine, 0, keepdims=False).astype(F32)
    segs = lax.dynamic_index_in_dim(segment_ids, mine, 0, keepdims=False)
    kind_col = kinds.reshape(length, 1)
    kind_row = kinds.reshape(1, length)
    first_seg = segs[::own]
    last_seg = segs[own - 1 :: own]
    lo = jnp.sum(segs[None, :] < first_seg[:, None], axis=1).astype(jnp.int32) // own
    hi = (
        jnp.sum(segs[None, :] <= last_seg[:, None], axis=1).astype(jnp.int32) + own - 1
    ) // own
    lane = lax.broadcasted_iota(jnp.int32, (length, LANES), 1)
    same = lane == segs[:, None]
    mq = jnp.where(same, FAR, 0.0).astype(BF16)
    mk = jnp.where(same | (lane >= DOCS), 0.0, -FAR).astype(BF16)

    vec_one = vec_all[:, : 7 * k_rows].reshape(devices, 7, k_rows).transpose(1, 0, 2)
    vec_one = vec_one.reshape(7, width)
    vecs = jnp.concatenate([vec_one[:6], jnp.zeros((2, width), F32)], axis=0)
    at = 7 * k_rows
    n_qb, n_ub = query_bias.shape[0], up_bias.shape[0]
    bias_q = vec_all[:, at : at + n_qb].reshape(2, 2 * width)
    bias_up = vec_all[:, at + n_qb : at + n_qb + n_ub].reshape(1, ff)
    bq = lax.dynamic_slice_in_dim(bias_q, me * 2 * feats, 2 * feats, 1)
    bv = lax.dynamic_slice_in_dim(vec_one[6:7], me * feats, feats, 1)

    at = 0
    wq_all = join_cols(bundle[:, at : at + q_blocks * q_rows], q_rows, q_blocks)
    at += q_blocks * q_rows
    wk_all = bundle[:, at : at + k_rows].reshape(width, width)
    at += k_rows
    wv_all = bundle[:, at : at + k_rows].reshape(width, width)
    at += k_rows
    wo = bundle[:, at : at + k_rows].reshape(width, width)
    at += k_rows
    wu = join_cols(bundle[:, at : at + u_blocks * u_rows], u_rows, u_blocks)
    at += u_blocks * u_rows
    wd = bundle[:, at : at + d_rows].reshape(ff, width)
    wq = lax.dynamic_slice_in_dim(wq_all, me * 2 * feats, 2 * feats, 1)
    wk = lax.dynamic_slice_in_dim(wk_all, me * feats, feats, 1)
    wv = lax.dynamic_slice_in_dim(wv_all, me * feats, feats, 1)

    q, kj, kjt, vx, vt = project(
        me_arr, xs, kind_col, kind_row, wq, wk, wv, bq, bv, groups, own, heads
    )
    att_rel, lse = attend(me_arr, lo, hi, q, mq, kj, mk, vt, groups, parts, own, heads)
    atts = [att_rel[0]] + [
        from_peer(att_rel[parts - step], step, parts) for step in range(1, parts)
    ]

    rows, gatt_rel, sum_up, sum_vec = feed(
        me_arr, atts, x_mine, ct, wo, wu, wd, bias_up, vecs, min(256, groups * own)
    )
    out_low, grad_first, att_nat, act, grad_up, normed_low, branch_two, branch_one = rows
    gatts = [gatt_rel[0]] + [
        from_peer(gatt_rel[parts - step], step, parts) for step in range(1, parts)
    ]
    grad_down = dot_tn(act, branch_two).astype(BF16)
    grad_upw = dot_tn(normed_low, grad_up).astype(BF16)
    grad_out = dot_tn(att_nat, branch_one).astype(BF16)
    vec_rows = 8
    feed_vec = jnp.concatenate(
        [
            sum_vec[:6].reshape(6, devices, k_rows).transpose(1, 0, 2).reshape(devices, -1),
            sum_up.reshape(devices, -1),
        ],
        axis=1,
    )
    feed_vec = jnp.pad(feed_vec, ((0, 0), (0, vec_rows * width - feed_vec.shape[1])))
    feed_chunks = jnp.concatenate(
        [
            grad_down.reshape(devices, d_rows, width),
            grad_upw.reshape(devices, u_rows, u_blocks, width)
            .transpose(0, 2, 1, 3)
            .reshape(devices, u_blocks * u_rows, width),
            grad_out.reshape(devices, k_rows, width),
            feed_vec.reshape(devices, vec_rows, width).astype(BF16),
        ],
        axis=1,
    )
    feed_sum = lax.psum_scatter(feed_chunks, everyone, scatter_dimension=0, tiled=False)

    dq, dk, dv = attend_back(
        me_arr, lo, hi, q, mq, kj, kjt, vx, mk, kind_col, lse, gatts, att_rel, own, heads
    )
    dx_rel, (gq, gk, gv, sum_q, sum_v) = unproject(
        me_arr, xs, kind_col, dq, dk, dv, grad_first, wq, wk, wv, groups, own
    )
    dx = dx_rel[0]
    for step in range(1, parts):
        dx = dx + from_peer(dx_rel[parts - step], step, parts).astype(F32)
    input_grad = to_groups(dx.astype(BF16).reshape(groups, own, width)).astype(F32)
    layer_output = to_groups(out_low.reshape(groups, own, width))

    places = devices // parts
    bias_full = jnp.zeros((2, 2 * width), F32)
    bias_full = lax.dynamic_update_slice_in_dim(bias_full, sum_q, me * 2 * feats, 1)
    value_full = jnp.zeros((1, width), F32)
    value_full = lax.dynamic_update_slice_in_dim(value_full, sum_v, me * feats, 1)
    att_vec = jnp.concatenate(
        [bias_full.reshape(devices, -1), value_full.reshape(devices, -1)], axis=1
    )
    wide = 2 * feats
    att_vec = jnp.pad(att_vec, ((0, 0), (0, vec_rows * wide - att_vec.shape[1])))
    att_chunks = jnp.concatenate(
        [
            gq.astype(BF16).reshape(devices, q_rows, wide),
            jnp.concatenate([gk, gv], axis=1).astype(BF16).reshape(devices, k_rows, wide),
            att_vec.reshape(devices, vec_rows, wide).astype(BF16),
        ],
        axis=1,
    )
    chunk_rows = att_chunks.shape[1]
    att_sum = lax.psum_scatter(
        att_chunks.reshape(places, parts * chunk_rows, wide),
        ("dp", "grp"),
        scatter_dimension=0,
        tiled=False,
    ).reshape(parts, chunk_rows, wide)
    by_cols = lax.all_to_all(att_sum, "hg", 0, 0, tiled=True).astype(F32)
    grad_query = by_cols[:, :q_rows].transpose(1, 0, 2).reshape(q_rows, 2 * width)
    kv = by_cols[:, q_rows : q_rows + k_rows]
    grad_key = kv[:, :, :feats].transpose(1, 0, 2).reshape(k_rows, width)
    grad_value = kv[:, :, feats:].transpose(1, 0, 2).reshape(k_rows, width)
    vec_own = jnp.sum(by_cols[:, q_rows + k_rows :], axis=0).reshape(-1)
    grad_query_bias = vec_own[:n_qb]
    grad_value_bias = vec_own[n_qb : n_qb + k_rows]

    feed_sum = feed_sum.astype(F32)
    grad_down_own = feed_sum[:d_rows]
    grad_up_own = jnp.concatenate(
        [
            feed_sum[d_rows + i * u_rows : d_rows + (i + 1) * u_rows]
            for i in range(u_blocks)
        ],
        axis=1,
    )
    at = d_rows + u_blocks * u_rows
    grad_out_own = feed_sum[at : at + k_rows]
    vec_two = feed_sum[at + k_rows :].reshape(-1)
    small = vec_two[: 6 * k_rows].reshape(6, k_rows)
    grad_up_bias = vec_two[6 * k_rows : 6 * k_rows + n_ub]
    return (
        layer_output,
        input_grad,
        grad_query,
        grad_query_bias,
        grad_key,
        grad_value,
        grad_value_bias,
        grad_out_own,
        small[0],
        small[1],
        small[2],
        grad_up_own,
        grad_up_bias,
        grad_down_own,
        small[3],
        small[4],
        small[5],
    )


def solution(mesh):
    dp, seq = mesh.shape["dp"], mesh.shape["seq"]

    def run(tokens, *rest):
        groups = tokens.shape[0] // dp
        parts = seq // groups
        fine = Mesh(mesh.devices.reshape(dp, groups, parts), ("dp", "grp", "hg"))
        block = P("dp", ("grp", "hg"), None)
        shared = P("dp", None)
        mat = P(("dp", "grp", "hg"), None)
        vec = P(("dp", "grp", "hg"))
        in_specs = (block, shared, shared, mat, vec, mat, mat, vec, mat, vec, vec, vec)
        in_specs += (mat, vec, mat, vec, vec, vec, block)
        out_specs = (block, block, mat, vec, mat, mat, vec, mat, vec, vec, vec)
        out_specs += (mat, vec, mat, vec, vec, vec)
        body = functools.partial(per_device, devices=dp * seq, parts=parts)
        return jax.shard_map(
            body, mesh=fine, in_specs=in_specs, out_specs=out_specs, check_vma=False
        )(tokens, *rest)

    return run
```

time: 1990 us -> 736 us (0.37)
  waiting for transfers between devices: 986 us -> 280 us
  matrix products: 531 us -> 19.9 us
  Pallas kernels: 0 us -> 208 us
  other arithmetic: 158 us -> 19.4 us
  local copies, waits for them, and re-layouts: 200 us -> 81.5 us
    dot_general x74 -> x3, matrix products: 531 us -> 19.9 us  [dot_tn(): lax.dot_general(a, b, (((0,), (0,)), ((), ())), preferred_element_type=F32)]
    reduce_scatter x5 -> x2, waiting for transfers between devices: 555 us -> 188 us  [the longest x1 141 us: per_device(): lax.psum_scatter(feed_chunks, everyone, scatter_dimension=0, tiled=False)]
    unnamed x16 -> x3, waiting for transfers between devices: 213 us -> 0.05 us
    pallas_call x0 -> x5, Pallas kernels: none -> 208 us  [the longest x1 70.6 us: attend_back(): pl.pallas_call(functools.partial(attend_back_body, parts, own, heads, blo...]
    all_gather x7 -> x1, waiting for transfers between devices: 219 us -> 70.8 us  [per_device(): bundle = lax.all_gather(pack, everyone, axis=0, tiled=False)]
    reduce_sum x19 -> x2, other arithmetic: 77.2 us -> 0.23 us  [the longest x1 0.22 us: per_device(): jnp.sum(segs[None, :] <= last_seg[:, None], axis=1).astype(jnp.int32) + own]
    slice x19 -> x18, local copies, waits for them, and re-layouts: 56.9 us -> 19.3 us  [the longest x1 11.1 us: per_device(): wd = bundle[:, at:at + d_rows].reshape(ff, width)]
    all_to_all x0 -> x2, blocking collectives: none -> 30.6 us  [the longest x1 25.6 us: per_device(): to_groups = lambda v: lax.all_to_all(v, 'grp', 0, 0, tiled=True)]
  transfers between devices with their start and end apart: 14 -> 10, of which waited for: 11 -> 5; matrix products, arithmetic and copies ran while one was open for 21% -> 13% of each run, Pallas kernels for 0% -> 10%
where the time goes in v1:
time: 736 us; the launch traced here: 727 us
  waiting for transfers between devices  280 us (38%)
  Pallas kernels  208 us (28%)
  blocking collectives  89.9 us (12%)
  local copies, waits for them, and re-layouts  81.5 us (11%)
  matrix products  19.9 us (3%)
  other arithmetic  19.4 us (3%)
  between operations  14.6 us (2%)
  starting transfers between devices  13.9 us (2%)
    reduce_scatter x1, waiting for transfers between devices, per_device(): lax.psum_scatter(feed_chunks, everyone, scatter_dimension=0, tiled=False)  141 us
    all_gather x1, waiting for transfers between devices, per_device(): bundle = lax.all_gather(pack, everyone, axis=0, tiled=False)  70.8 us
    pallas_call x1, Pallas kernels, attend_back(): pl.pallas_call(functools.partial(attend_back_body, parts, own, heads, blo...  70.6 us
    unnamed x1, blocking collectives  59.3 us
    pallas_call x1, Pallas kernels, attend(): pl.pallas_call(functools.partial(attend_body, parts, own, heads), grid_sp...  57.7 us
    reduce_scatter x1, waiting for transfers between devices, per_device(): lax.psum_scatter(att_chunks.reshape(places, parts * chunk_rows, wide), ('...  46.8 us
    pallas_call x1, Pallas kernels, feed(): pl.pallas_call(functools.partial(feed_body, parts, feats), grid_spec=grid...  40 us
    all_to_all x1, blocking collectives, per_device(): to_groups = lambda v: lax.all_to_all(v, 'grp', 0, 0, tiled=True)  25.6 us
  transfers between devices with their start and end apart: 10, of which 5 were waited for; matrix products, arithmetic and copies ran while one was open for 13% of the time, Pallas kernels for 10%

profile of v1, /device:TPU:0, one launch (start us, length us, event | category | flops | bytes accessed | tf_op | source)
XLA Modules:
  0.0 726.9 jit_solution(16236936589619429572)
XLA Ops:
  7.4 0.9 slice_dynamic-update-slice_fusion.1
  8.3 0.9 slice_dynamic-update-slice_fusion
  9.2 0.8 constant_dynamic-update-slice_fusion.3
  10.7 0.8 constant_dynamic-update-slice_fusion.1
  14.6 0.9 constant_dynamic-update-slice_fusion
  15.5 0.8 copy-done.9
  16.3 5.2 all-to-all-start
  21.9 59.3 %all-reduce.3 = bf16[11520]{0:T(1024)(128)(2,1)S(1)} all-reduce(bf16[11520]{0:T(1024)(128)(2,1)S(1)} %dynamic-update-slice), channel_id=3, replica_groups=mesh['dp'=4,'grp'=4,'hg'=2] {'dp','grp','hg'}, use_global_device_ids=true, to_apply=%add.3 | all-reduce | flops 11520 | bytes 46080
  82.0 1.4 copy.75.refs_2_.refs_6_
  85.3 1.2 select_convert_fusion
  86.6 3.6 all-to-all-start.1
  91.4 70.8 %all-gather.4.cloned.1.call-done = bf16[11520,768]{1,0:T(8,128)(2,1)} async-done(((bf16[360,768]{1,0:T(8,128)(2,1)}), bf16[11520,768]{1,0:T(8,128)(2,1)}) %all-gather.4.cloned.1.call-update) | async-done | bytes 17694736 | tf_op jit(solution)/shard_map/all_gather | solution.py:637
  162.2 11.1 %fusion.7 = (bf16[32,96,768]{2,1,0:T(8,128)(2,1)}, bf16[32,96,768]{2,1,0:T(8,128)(2,1)}, bf16[32,96,768]{2,1,0:T(8,128)(2,1)}) fusion(bf16[32,360,768]{2,1,0:T(8,128)(2,1)} %bitcast.84), kind=kLoop, calls=%fused_computation.63 | loop fusion | bytes 28311552 | tf_op jit(solution)/shard_map/slice | solution.py:684
  173.4 9.2 %copy.74 = bf16[32,2,48,768]{3,1,2,0:T(2,128)(2,1)} copy(bf16[32,2,48,768]{3,2,1,0:T(8,128)(2,1)} %bitcast.77) | data formatting | bytes 9437184 | tf_op jit(solution)/shard_map/reshape | solution.py:582
  182.5 3.3 copy.89
  185.8 3.3 fusion.8
  189.1 1.1 constant_dynamic-slice_fusion.2
  190.2 1.5 constant_dynamic-slice_fusion.4.refs_4_.refs_7_
  191.7 14.2 %project.1 = (bf16[2048,768]{1,0:T(8,128)(2,1)}, bf16[2048,768]{1,0:T(8,128)(2,1)}, bf16[768,2048]{1,0:T(8,128)(2,1)}, bf16[2048,768]{1,0:T(8,128)(2,1)}, bf16[384,2048]{1,0:T(8,128)(2,1)}) custom-call(s32[1]{0:T(128)} %bitcast.me_ref, bf16[1024,768]{1,0:T(8,128)(2,1)} %bitcast.71, bf16[1024,768]{1,0:T(8,128)(2,1)} %collective-permute-done.refs_1_, ...), custom_call_target="tpu_custom_call" | custom-call | tf_op jit(solution)/shard_map/project/pallas_call | solution.py:114
  206.0 57.7 %attend.1 = (bf16[1024,384]{1,0:T(8,128)(2,1)}, bf16[1024,384]{1,0:T(8,128)(2,1)}, f32[8,2048]{1,0:T(8,128)}) custom-call(s32[1]{0:T(128)} %bitcast.me_ref, s32[8]{0:T(128)} %get-tuple-element.103.lo_ref, s32[8]{0:T(128)} %get-tuple-element.102.hi_ref, bf16[2048,768]{1,0:T(8,128)(2,1)} %get-tuple-element.47.refs_0_, ...), custom_call_target="tpu_custom_call" | custom-call | tf_op jit(solution)/shard_map/attend/pallas_call | solution.py:204
  265.4 4.7 copy.76
  270.1 3.2 copy.90
  273.3 1.1 copy-done.3
  274.7 40.0 %feed.1 = (bf16[1024,768]{1,0:T(8,128)(2,1)}, f32[1024,768]{1,0:T(8,128)}, bf16[1024,768]{1,0:T(8,128)(2,1)}, bf16[1024,3072]{1,0:T(8,128)(2,1)}, bf16[1024,3072...) custom-call(s32[1]{0:T(128)} %bitcast.me_ref, ...), custom_call_target="tpu_custom_call" | custom-call | tf_op jit(solution)/shard_map/feed/pallas_call | solution.py:461
  314.9 2.3 collective-permute-done.2.refs_9_
  317.2 0.9 copy-done.8
  318.1 70.6 %attend_back.1 = (bf16[2048,768]{1,0:T(8,128)(2,1)}, bf16[2048,384]{1,0:T(8,128)(2,1)}, bf16[2048,384]{1,0:T(8,128)(2,1)}) custom-call(s32[1]{0:T(128)} %bitcast.me_ref, s32[8]{0:T(128)} %get-tuple-element.103.lo_ref, s32[8]{0:T(128)} %get-tuple-element.102.hi_ref, bf16[2048,768]{1,0:T(8,128)(2,1)} %get-tuple-element.47.refs_0_, ...), custom_call_target="tpu_custom_call" | custom-call | tf_op jit(solution)/shard_map/attend_back/pallas_call | solution.py:341
  388.7 25.1 %unproject.1 = (f32[1024,768]{1,0:T(8,128)}, bf16[1024,768]{1,0:T(8,128)(2,1)}, f32[1536,768]{1,0:T(8,128)}, f32[768,384]{1,0:T(8,128)}, f32[768,384]{1,0:T(8,128)}, /*index=5*/f32[2,768]{1,0:T(2,128)}, f32[1,384]{1,0:T(1,128)}) custom-call(s32[1]{0:T(128)} %bitcast.me_ref, bf16[1024,768]{1,0:T(8,128)(2,1)} %bitcast.73, ...), custom_call_target="tpu_custom_call" | custom-call | tf_op jit(solution)/shard_map/unproject/pallas_call | solution.py:551
  415.6 2.7 convert_element_type.81
  418.7 2.1 pad_maximum_fusion.1
  420.9 1.3 copy-done.25
  422.2 9.7 %convolution_convert_fusion = bf16[768,3072]{1,0:T(8,128)(2,1)} fusion(bf16[1024,768]{1,0:T(8,128)(2,1)S(1)} %copy-done.25, bf16[1024,3072]{1,0:T(8,128)(2,1)} %get-tuple-element.72), kind=kOutput, calls=%fused_computation.1 | convolution fusion | flops 4834197504 | bytes 12582912 | tf_op jit(solution)/shard_map/dot_general | solution.py:37
  431.9 9.8 %reshape.215 = bf16[32,24,4,768]{3,2,1,0:T(4,128)(2,1)} reshape(bf16[768,3072]{1,0:T(8,128)(2,1)} %convolution_convert_fusion) | data formatting | bytes 9437184 | tf_op jit(solution)/shard_map/reshape | solution.py:719
  441.7 5.7 copy.83
  448.1 1.4 convolution_convert_fusion.2
  449.6 8.8 %convolution_convert_fusion.1 = bf16[3072,768]{1,0:T(8,128)(2,1)S(1)} fusion(bf16[1024,3072]{1,0:T(8,128)(2,1)} %get-tuple-element.69, bf16[1024,768]{1,0:T(8,128)(2,1)S(1)} %copy-done.22), kind=kOutput, calls=%fused_computation.2 | convolution fusion | flops 4834197504 | bytes 12582912 | tf_op jit(solution)/shard_map/dot_general | solution.py:37
  458.4 5.1 pad_maximum_fusion
  463.8 3.6 all-to-all-start.2
  467.4 1.1 copy-done.4
  468.5 2.7 add_convert_fusion
  471.2 19.3 %all-to-all-done.2 = bf16[4,256,768]{2,1,0:T(8,128)(2,1)S(1)} async-done(((bf16[4,256,768]{2,1,0:T(8,128)(2,1)}), bf16[4,256,768]{2,1,0:T(8,128)(2,1)S(1)}, u32[]{:S(2)}, u32[]{:S(2)}) %all-to-all-start.2) | async-done | bytes 1572896 | tf_op jit(solution)/shard_map/all_to_all | solution.py:644
  490.6 25.6 %all_to_all.26 = bf16[4,256,768]{2,1,0:T(8,128)(2,1)S(1)} all-to-all(bf16[4,256,768]{2,1,0:T(8,128)(2,1)S(1)} %bitcast.90), channel_id=1, replica_groups=mesh['dp'=4,'grp'=4,'hg'=2] {'grp'}, dimensions={0} | all-to-all | bytes 3145728 | tf_op jit(solution)/shard_map/all_to_all | solution.py:644
  516.2 1.9 convert_element_type.80
  518.1 46.8 %reduce-scatter.3.cloned.1.call-done = bf16[1,160,768]{2,1,0:T(8,128)(2,1)} async-done(((bf16[16,160,768]{2,1,0:T(8,128)(2,1)}), bf16[1,160,768]{2,1,0:T(8,128)(2,1)}) %reduce-scatter.3.cloned.1.call-update) | async-done | bytes 245776 | tf_op jit(solution)/shard_map/reduce_scatter | solution.py:760
  564.9 5.0 all_to_all.25
  573.1 140.8 %reduce-scatter.5.cloned.1.call-done = bf16[1,224,768]{2,1,0:T(8,128)(2,1)} async-done(((bf16[32,224,768]{2,1,0:T(8,128)(2,1)}), bf16[1,224,768]{2,1,0:T(8,128)(2,1)}) %reduce-scatter.5.cloned.1.call-update) | async-done | bytes 344080 | tf_op jit(solution)/shard_map/reduce_scatter | solution.py:727
  713.9 1.0 convert_element_type.88
  719.0 1.1 copy.106
  (132 shorter events, 20.7 us)
Async XLA Ops:
  7.2 74.3 %copy-start = (s32[4,2048]{1,0:T(4,128)S(1)}, s32[4,2048]{1,0:T(4,128)}, u32[]{:S(2)}) copy-start(s32[4,2048]{1,0:T(4,128)} %param.21) | copy-start | bytes 98308
  7.2 14.3 %copy-start.20 = (bf16[96]{0:T(256)(128)(2,1)S(1)}, bf16[96]{0:T(256)(128)(2,1)}, u32[]{:S(2)}) copy-start(bf16[96]{0:T(256)(128)(2,1)} %param.23) | copy-start | bytes 580
  7.2 14.3 %copy-start.19 = (bf16[24]{0:T(256)(128)(2,1)S(1)}, bf16[24]{0:T(256)(128)(2,1)}, u32[]{:S(2)}) copy-start(bf16[24]{0:T(256)(128)(2,1)} %param.26) | copy-start | bytes 148
  7.2 14.3 %copy-start.13 = (bf16[24]{0:T(256)(128)(2,1)S(1)}, bf16[24]{0:T(256)(128)(2,1)}, u32[]{:S(2)}) copy-start(bf16[24]{0:T(256)(128)(2,1)} %param.28) | copy-start | bytes 148
  7.2 14.3 %copy-start.14 = (bf16[24]{0:T(256)(128)(2,1)S(1)}, bf16[24]{0:T(256)(128)(2,1)}, u32[]{:S(2)}) copy-start(bf16[24]{0:T(256)(128)(2,1)} %param.29) | copy-start | bytes 148
  7.2 14.3 %copy-start.15 = (bf16[24]{0:T(256)(128)(2,1)S(1)}, bf16[24]{0:T(256)(128)(2,1)}, u32[]{:S(2)}) copy-start(bf16[24]{0:T(256)(128)(2,1)} %param.30) | copy-start | bytes 148
  7.3 14.3 %copy-start.21 = (bf16[96]{0:T(256)(128)(2,1)S(1)}, bf16[96]{0:T(256)(128)(2,1)}, u32[]{:S(2)}) copy-start(bf16[96]{0:T(256)(128)(2,1)} %param.32) | copy-start | bytes 580
  7.3 14.3 %copy-start.16 = (bf16[24]{0:T(256)(128)(2,1)S(1)}, bf16[24]{0:T(256)(128)(2,1)}, u32[]{:S(2)}) copy-start(bf16[24]{0:T(256)(128)(2,1)} %param.34) | copy-start | bytes 148
  7.3 14.3 %copy-start.17 = (bf16[24]{0:T(256)(128)(2,1)S(1)}, bf16[24]{0:T(256)(128)(2,1)}, u32[]{:S(2)}) copy-start(bf16[24]{0:T(256)(128)(2,1)} %param.35) | copy-start | bytes 148
  7.3 14.3 %copy-start.18 = (bf16[24]{0:T(256)(128)(2,1)S(1)}, bf16[24]{0:T(256)(128)(2,1)}, u32[]{:S(2)}) copy-start(bf16[24]{0:T(256)(128)(2,1)} %param.36) | copy-start | bytes 148
  7.3 74.2 %copy-start.11 = (s32[4,2048]{1,0:T(4,128)S(1)}, s32[4,2048]{1,0:T(4,128)}, u32[]{:S(2)}) copy-start(s32[4,2048]{1,0:T(4,128)} %param.20) | copy-start | bytes 98308
  7.3 154.9 %all-gather.4.cloned.1.call-start = ((), (), s32[]{:S(2)}) async-start(), calls=%async_computation.9 | async-start | bytes 18247680 | tf_op jit(solution)/shard_map/all_gather | solution.py:637
  15.5 0.8 copy-start.9
  16.3 70.3 %all-to-all-start = ((bf16[4,256,768]{2,1,0:T(8,128)(2,1)}), bf16[4,256,768]{2,1,0:T(8,128)(2,1)S(1)}, u32[]{:S(2)}, u32[]{:S(2)}) async-start(bf16[4,256,768]{2,1,0:T(8,128)(2,1)} %param.19), calls=%async_computation | async-start | bytes 3145728 | tf_op jit(solution)/shard_map/all_to_all | solution.py:644
  86.6 86.8 %copy-start.2 = (bf16[4,256,768]{2,1,0:T(8,128)(2,1)}, bf16[4,256,768]{2,1,0:T(8,128)(2,1)S(1)}, u32[]{:S(2)}) copy-start(bf16[4,256,768]{2,1,0:T(8,128)(2,1)S(1)} %all-to-all-done) | copy-start | bytes 4718596
  86.6 186.7 %all-to-all-start.1 = ((bf16[4,256,768]{2,1,0:T(8,128)(2,1)}), bf16[4,256,768]{2,1,0:T(8,128)(2,1)S(1)}, u32[]{:S(2)}, u32[]{:S(2)}) async-start(bf16[4,256,768]{2,1,0:T(8,128)(2,1)} %param.37), calls=%async_computation.1 | async-start | bytes 3145728 | tf_op jit(solution)/shard_map/all_to_all | solution.py:644
  90.2 474.8 %reduce-scatter.3.cloned.1.call-start = ((), (), s32[]{:S(2)}) async-start(), calls=%async_computation.7 | async-start | bytes 4177920 | tf_op jit(solution)/shard_map/reduce_scatter | solution.py:760
  90.7 101.0 %collective-permute-start = (bf16[1024,768]{1,0:T(8,128)(2,1)S(1)}, bf16[1024,768]{1,0:T(8,128)(2,1)}, u32[]{:S(2)}, u32[]{:S(2)}) collective-permute-start(bf16[1024,768]{1,0:T(8,128)(2,1)S(1)} %bitcast.70), channel_id=1, source_target_pairs={{1,0},{0,1},{3,2},{2,3},{5,4},{4,5},{7,6},{6,7},{9,8},{8,9},{11,10... | collective-permute-start | bytes 4718600 | tf_op jit(solution)/shard_map/ppermute | solution.py:570
  263.7 9.6 %collective-permute-start.1 = (bf16[1024,384]{1,0:T(8,128)(2,1)}, bf16[1024,384]{1,0:T(8,128)(2,1)S(1)}, u32[]{:S(2)}, u32[]{:S(2)}) collective-permute-start(bf16[1024,384]{1,0:T(8,128)(2,1)} %get-tuple-element.51.refs_11_), channel_id=1, source_target_pairs={{1,0},{0,1},{3,2},{2,3},{5,4},{4,5},{7,6},{6,7},{9,8},{8,9},{11,10... | collective-permute-start | bytes 2359304 | tf_op jit(solution)/shard_map/ppermute | solution.py:570
  273.3 1.2 copy-start.3
  273.3 1.4 copy-start.7
  314.7 2.6 collective-permute-start.2
  317.2 0.9 copy-start.8
  415.5 2.7 copy-start.6
  415.6 3.0 copy-start.5
  420.8 1.4 copy-start.25
  420.8 293.1 %reduce-scatter.5.cloned.1.call-start = ((), (), s32[]{:S(2)}) async-start(), calls=%async_computation.8 | async-start | bytes 11354112 | tf_op jit(solution)/shard_map/reduce_scatter | solution.py:727
  441.7 5.7 copy-start.12
  441.7 6.0 copy-start.10
  441.7 6.3 copy-start.23
  441.7 6.3 copy-start.24
  448.1 1.5 copy-start.22
  449.5 8.8 %slice-start = ((s8[4718592]{0:T(1024)(128)(4,1)}), s8[4194304]{0:T(1024)(128)(4,1)S(1)}, s32[]{:S(2)}) async-start(s8[4718592]{0:T(1024)(128)(4,1)} %bitcast.81), calls=%async_computation.10 | async-start | bytes 8388608
  449.5 8.8 %slice-start.1 = ((s8[4718592]{0:T(1024)(128)(4,1)}), s8[524288]{0:T(1024)(128)(4,1)S(1)}, s32[]{:S(2)}) async-start(s8[4718592]{0:T(1024)(128)(4,1)} %bitcast.81), calls=%async_computation.11 | async-start | bytes 1048576
  463.5 3.8 collective-permute-start.3
  463.8 26.8 %all-to-all-start.2 = ((bf16[4,256,768]{2,1,0:T(8,128)(2,1)}), bf16[4,256,768]{2,1,0:T(8,128)(2,1)S(1)}, u32[]{:S(2)}, u32[]{:S(2)}) async-start(bf16[4,256,768]{2,1,0:T(8,128)(2,1)} %bitcast.15), calls=%async_computation.2 | async-start | bytes 3145728 | tf_op jit(solution)/shard_map/all_to_all | solution.py:644
  467.4 1.1 copy-start.4
  572.5 147.7 %copy-start.1 = (s32[4,2048]{1,0:T(4,128)S(1)}, s32[4,2048]{1,0:T(4,128)}, u32[]{:S(2)}) copy-start(s32[4,2048]{1,0:T(4,128)} %param.21) | copy-start | bytes 98308
Sparse Core Ops, SparseCore 0:
  16.4 145.7 all-gather.3
  420.9 143.9 reduce-scatter.2
  570.9 142.9 reduce-scatter.4
